TPU v7x, 256 devices: a whole 4x4x8 slice. The times are simulated.
256 devices in a mesh: dom: 32 (over z_lo, y, x), ch: 8 (over z_hi, core).
Axes of the slice: x: 4, y: 4, z: 8 (z_hi: 4, z_lo: 2; z = z_hi * 2 + z_lo), core: 2. Of those that a mesh axis runs over, the one named last changes fastest.
Arguments:
- node_feats: bfloat16 [512, 24576], P('ch', 'dom'), may hold values from -6 to 6
- edge_feats: bfloat16 [512, 32768], P('ch', 'dom'), may hold values from -6 to 6
- send_rows: int32 [32768], P('dom'), may hold values from 0 to 767
- edge_src: int32 [32768], P('dom'), may hold values from 0 to 1791
- edge_dst: int32 [32768], P('dom'), may hold values from 0 to 767
- w_edge_in: bfloat16 [2, 3, 512, 512], P(None, None, None, 'ch'), may hold values from -0.15625 to 0.15625
- w_edge_out: bfloat16 [2, 512, 512], P(None, 'ch'), may hold values from -0.25 to 0.25
- w_node_in: bfloat16 [2, 2, 512, 512], P(None, None, None, 'ch'), may hold values from -0.1875 to 0.1875
- w_node_out: bfloat16 [2, 512, 512], P(None, 'ch'), may hold values from -0.25 to 0.25
Outputs:
- nodes_out: bfloat16 [512, 24576], P('ch', 'dom')
- edges_out: bfloat16 [512, 32768], P('ch', 'dom')
All inputs are finite; a program needn't handle non-finite values.
Results may differ from a plain program's by a relative error of at most 0.0085.
Values may be sent and summed in bfloat16 or wider, within the bound.
No kernel may reach another device: no remote copies, remote signals or barrier semaphores. Data moves between devices by JAX's collectives and lax.ppermute only.
A program may use at most 64 MiB of HBM per device.

v0:
```python
import jax
import jax.numpy as jnp
from jax import lax
from jax.sharding import PartitionSpec as P

LATENT = 512
SLOTS = 32
LAYERS = 2


def finish(hidden, weight_out, residual):
    summed = lax.psum_scatter(
        lax.dot_general(
            weight_out, hidden, (((0,), (0,)), ((), ())), preferred_element_type=jnp.float32
        ),
        "ch",
        scatter_dimension=0,
        tiled=True,
    )
    total, squares = lax.psum((jnp.sum(summed, axis=0), jnp.sum(summed * summed, axis=0)), "ch")
    mean = total / LATENT
    var = squares / LATENT - mean * mean
    normed = (summed - mean) * lax.rsqrt(var + 1e-05)
    return (residual.astype(jnp.float32) + normed).astype(jnp.bfloat16)


def edge_hidden(stacked, weight_in):
    return jnp.einsum(
        "akh,ake->he",
        weight_in,
        lax.all_gather(stacked, "ch", axis=1, tiled=True),
        preferred_element_type=jnp.float32,
    )


def shards(
    node_feats,
    edge_feats,
    send_rows,
    edge_src,
    edge_dst,
    w_edge_in,
    w_edge_out,
    w_node_in,
    w_node_out,
):
    share = node_feats.shape[0]
    node_count = node_feats.shape[1]
    domains = lax.axis_size("dom")
    nodes = node_feats
    edges = edge_feats
    for layer in range(LAYERS):
        packed = nodes[:, send_rows].reshape(share, domains, SLOTS)
        received = lax.all_to_all(packed, "dom", split_axis=1, concat_axis=1, tiled=True).reshape(
            share, domains * SLOTS
        )
        extended = jnp.concatenate([nodes, received], axis=1)
        stacked = jnp.stack([edges, extended[:, edge_src], nodes[:, edge_dst]])
        hidden = jax.nn.silu(edge_hidden(stacked, w_edge_in[layer])).astype(jnp.bfloat16)
        edges = finish(hidden, w_edge_out[layer], edges)
        gathered = (
            jnp.zeros((share, node_count), jnp.float32)
            .at[:, edge_dst]
            .add(edges.astype(jnp.float32))
        )
        both = jnp.stack([nodes, gathered.astype(jnp.bfloat16)])
        node_weight = w_node_in[layer]
        hidden_n = jnp.einsum(
            "akh,akn->hn",
            node_weight,
            lax.all_gather(both, "ch", axis=1, tiled=True),
            preferred_element_type=jnp.float32,
        )
        hidden_n = jax.nn.silu(hidden_n).astype(jnp.bfloat16)
        nodes = finish(hidden_n, w_node_out[layer], nodes)
    return (nodes, edges)


def solution(mesh):
    in_specs = (
        P("ch", "dom"),
        P("ch", "dom"),
        P("dom"),
        P("dom"),
        P("dom"),
        P(None, None, None, "ch"),
        P(None, "ch", None),
        P(None, None, None, "ch"),
        P(None, "ch", None),
    )
    out_specs = (P("ch", "dom"), P("ch", "dom"))
    return jax.shard_map(shards, mesh=mesh, in_specs=in_specs, out_specs=out_specs, check_vma=False)
```

profile of v0, /device:TPU:42, one launch (start us, length us, event | category | flops | bytes accessed | tf_op | source)
XLA Modules:
  0.0 487.1 jit_solution(14797563048734557695)
XLA Ops:
  7.9 1.1 copy.23
  8.9 3.2 gather_fusion
  12.2 0.8 reshape.116
  13.0 8.4 %all-to-all-start = ((bf16[32,2,1024]{2,1,0:T(2,128)(2,1)}), bf16[32,2,1024]{2,1,0:T(2,128)(2,1)S(1)}, u32[]{:S(2)}, u32[]{:S(2)}) async-start(bf16[32,2,1024]{2,1,0:T(2,128)(2,1)} %reshape.116), calls=%async_computation | async-start | bytes 262144 | tf_op jit(solution)/shard_map/all_to_all | solution.py:54
  21.5 3.2 gather_fusion.2
  24.9 2.0 all-to-all-done
  27.2 3.2 gather_fusion.1
  30.6 0.8 pad_maximum_fusion.3
  31.4 43.4 %all-gather.5.cloned.1.call-done = bf16[3,512,1024]{2,1,0:T(8,128)(2,1)} async-done(((bf16[3,64,1024]{2,1,0:T(8,128)(2,1)}), bf16[3,512,1024]{2,1,0:T(8,128)(2,1)}) %all-gather.5.cloned.1.call-update) | async-done | bytes 3145744 | tf_op jit(solution)/shard_map/all_gather | solution.py:31
  74.8 2.9 convolution_bitcast_fusion.1
  77.7 1.9 copy.36
  79.9 42.3 %reduce-scatter.13.cloned.1.call-done = f32[64,1024]{1,0:T(8,128)} async-done(((f32[512,1024]{1,0:T(8,128)}), f32[64,1024]{1,0:T(8,128)}) %reduce-scatter.13.cloned.1.call-update) | async-done | bytes 262160
  122.2 1.1 copy.37
  123.6 1.0 reduce_sum.72
  124.6 18.0 %all-reduce.3 = (f32[1024]{0:T(1024)S(1)}, f32[1024]{0:T(1024)S(1)}) all-reduce(f32[1024]{0:T(1024)S(1)} %multiply_reduce_fusion.1, f32[1024]{0:T(1024)S(1)} %reduce_sum.72), channel_id=1, replica_groups=mesh['dom'=32,'ch'=8] {'ch'}, use_global_device_ids=true, to_apply=%region_4.5 | all-reduce | flops 2048 | bytes 16384 | tf_op jit(solution)/shard_map/psum | solution.py:20
  142.9 6.2 %scatter_custom_fusion = f32[64,768]{0,1:T(8,128)S(1)} fusion(s32[1024]{0:T(1024)S(1)} %get-tuple-element.23, bf16[64,1024]{0,1:T(8,128)(2,1)S(1)} %add_convert_fusion, f32[]{:T(128)} %constant.23.clone.1), kind=kCustom, calls=%fused_computation.21 | custom fusion | flops 131072 | bytes 458756 | tf_op jit(solution)/shard_map/scatter-add | solution.py:64
  150.0 33.0 %all-gather.7.cloned.1.call-done = bf16[2,512,768]{2,1,0:T(8,128)(2,1)} async-done(((bf16[2,64,768]{2,1,0:T(8,128)(2,1)}), bf16[2,512,768]{2,1,0:T(8,128)(2,1)}) %all-gather.7.cloned.1.call-update) | async-done | bytes 1572880 | tf_op jit(solution)/shard_map/all_gather | solution.py:71
  183.0 2.2 convolution_bitcast_fusion.3
  185.2 1.6 copy.38
  186.8 39.2 %reduce-scatter.15.cloned.1.call-done = f32[64,768]{1,0:T(8,128)} async-done(((f32[512,768]{1,0:T(8,128)}), f32[64,768]{1,0:T(8,128)}) %reduce-scatter.15.cloned.1.call-update) | async-done | bytes 196624
  226.0 1.1 copy.39
  227.3 1.0 reduce_sum.74
  228.2 16.3 %all-reduce.2 = (f32[768]{0:T(1024)S(1)}, f32[768]{0:T(1024)S(1)}) all-reduce(f32[768]{0:T(1024)S(1)} %multiply_reduce_fusion.3, f32[768]{0:T(1024)S(1)} %reduce_sum.74), channel_id=1, replica_groups=mesh['dom'=32,'ch'=8] {'ch'}, use_global_device_ids=true, to_apply=%region_10.11 | all-reduce | flops 1536 | bytes 12288 | tf_op jit(solution)/shard_map/psum | solution.py:20
  244.9 3.2 gather_fusion.3
  248.1 0.8 reshape.118
  248.9 8.5 %all-to-all-start.1 = ((bf16[32,2,1024]{2,1,0:T(2,128)(2,1)}), bf16[32,2,1024]{2,1,0:T(2,128)(2,1)S(1)}, u32[]{:S(2)}, u32[]{:S(2)}) async-start(bf16[32,2,1024]{2,1,0:T(2,128)(2,1)} %reshape.118), calls=%async_computation.1 | async-start | bytes 262144 | tf_op jit(solution)/shard_map/all_to_all | solution.py:54
  257.5 3.2 gather_fusion.5
  260.7 2.2 all-to-all-done.1
  263.2 3.2 gather_fusion.4
  266.6 1.0 copy.31
  267.7 41.0 %all-gather.9.cloned.1.call-done = bf16[3,512,1024]{2,1,0:T(8,128)(2,1)} async-done(((bf16[3,64,1024]{2,1,0:T(8,128)(2,1)}), bf16[3,512,1024]{2,1,0:T(8,128)(2,1)}) %all-gather.9.cloned.1.call-update) | async-done | bytes 3145744 | tf_op jit(solution)/shard_map/all_gather | solution.py:31
  308.7 2.9 convolution_bitcast_fusion
  311.6 1.9 copy.40
  313.5 42.5 %reduce-scatter.17.cloned.1.call-done = f32[64,1024]{1,0:T(8,128)} async-done(((f32[512,1024]{1,0:T(8,128)}), f32[64,1024]{1,0:T(8,128)}) %reduce-scatter.17.cloned.1.call-update) | async-done | bytes 262160
  356.1 1.1 copy.41
  357.4 1.0 reduce_sum.76
  358.4 18.4 %all-reduce.1 = (f32[1024]{0:T(1024)S(1)}, f32[1024]{0:T(1024)S(1)}) all-reduce(f32[1024]{0:T(1024)S(1)} %multiply_reduce_fusion, f32[1024]{0:T(1024)S(1)} %reduce_sum.76), channel_id=1, replica_groups=mesh['dom'=32,'ch'=8] {'ch'}, use_global_device_ids=true, to_apply=%region_15.16 | all-reduce | flops 2048 | bytes 16384 | tf_op jit(solution)/shard_map/psum | solution.py:20
  377.2 6.2 %scatter_custom_fusion.1 = f32[64,768]{0,1:T(8,128)S(1)} fusion(s32[1024]{0:T(1024)S(1)} %get-tuple-element.23, bf16[64,1024]{0,1:T(8,128)(2,1)S(1)} %fusion.6, f32[]{:T(128)} %constant.23.clone.1), kind=kCustom, calls=%fused_computation.23 | custom fusion | flops 131072 | bytes 458756 | tf_op jit(solution)/shard_map/scatter-add | solution.py:64
  383.5 0.9 copy.32
  384.4 32.9 %all-gather.11.cloned.1.call-done = bf16[2,512,768]{2,0,1:T(2,128)(2,1)} async-done(((bf16[2,64,768]{2,0,1:T(2,128)(2,1)}), bf16[2,512,768]{2,0,1:T(2,128)(2,1)}) %all-gather.11.cloned.1.call-update) | async-done | bytes 1572880 | tf_op jit(solution)/shard_map/all_gather | solution.py:71
  417.3 2.2 convolution_bitcast_fusion.2
  419.5 1.6 copy.42
  421.1 0.8 copy.35
  421.9 38.7 %reduce-scatter.19.cloned.1.call-done = f32[64,768]{1,0:T(8,128)} async-done(((f32[512,768]{1,0:T(8,128)}), f32[64,768]{1,0:T(8,128)}) %reduce-scatter.19.cloned.1.call-update) | async-done | bytes 196624
  460.6 1.1 copy.43
  461.9 1.0 reduce_sum.78
  462.8 16.3 %all-reduce = (f32[768]{0:T(1024)S(1)}, f32[768]{0:T(1024)S(1)}) all-reduce(f32[768]{0:T(1024)S(1)} %multiply_reduce_fusion.2, f32[768]{0:T(1024)S(1)} %reduce_sum.78), channel_id=1, replica_groups=mesh['dom'=32,'ch'=8] {'ch'}, use_global_device_ids=true, to_apply=%region_21.22 | all-reduce | flops 1536 | bytes 12288 | tf_op jit(solution)/shard_map/psum | solution.py:20
  479.4 0.8 copy.34
  (61 shorter events, 5.4 us)
Async XLA Ops:
  7.2 14.3 %copy-start.7 = (s32[1024]{0:T(1024)S(1)}, s32[1024]{0:T(1024)}, u32[]{:S(2)}) copy-start(s32[1024]{0:T(1024)} %param.13) | copy-start | bytes 12292
  8.9 16.0 %copy-start.8 = (s32[1024]{0:T(1024)S(1)}, s32[1024]{0:T(1024)}, u32[]{:S(2)}) copy-start(s32[1024]{0:T(1024)} %param.12) | copy-start | bytes 12292
  13.0 13.9 %all-to-all-start = ((bf16[32,2,1024]{2,1,0:T(2,128)(2,1)}), bf16[32,2,1024]{2,1,0:T(2,128)(2,1)S(1)}, u32[]{:S(2)}, u32[]{:S(2)}) async-start(bf16[32,2,1024]{2,1,0:T(2,128)(2,1)} %reshape.116), calls=%async_computation | async-start | bytes 262144 | tf_op jit(solution)/shard_map/all_to_all | solution.py:54
  21.4 53.4 %all-gather.5.cloned.1.call-start = ((), (), s32[]{:S(2)}) async-start(), calls=%async_computation.6 | async-start | bytes 3538944 | tf_op jit(solution)/shard_map/all_gather | solution.py:31
  24.7 5.8 %copy-start = (bf16[64,1024]{1,0:T(8,128)(2,1)S(1)}, bf16[64,1024]{1,0:T(8,128)(2,1)}, u32[]{:S(2)}) copy-start(bf16[64,1024]{1,0:T(8,128)(2,1)} %param.10) | copy-start | bytes 393220
  27.2 47.6 %copy-start.1 = (bf16[2,3,512,64]{2,3,1,0:T(8,128)(2,1)S(1)}, bf16[2,3,512,64]{2,3,1,0:T(8,128)(2,1)}, u32[]{:S(2)}) copy-start(bf16[2,3,512,64]{2,3,1,0:T(8,128)(2,1)} %param.14) | copy-start | bytes 1179652
  27.2 47.6 %copy-start.4 = (bf16[2,64,512]{2,1,0:T(8,128)(2,1)S(1)}, bf16[2,64,512]{2,1,0:T(8,128)(2,1)}, u32[]{:S(2)}) copy-start(bf16[2,64,512]{2,1,0:T(8,128)(2,1)} %param.15) | copy-start | bytes 393220
  31.4 90.8 %reduce-scatter.13.cloned.1.call-start = ((), (), s32[]{:S(2)}) async-start(), calls=%async_computation.10 | async-start | bytes 2359296
  79.6 103.3 %all-gather.7.cloned.1.call-start = ((), (), s32[]{:S(2)}) async-start(), calls=%async_computation.7 | async-start | bytes 1769472 | tf_op jit(solution)/shard_map/all_gather | solution.py:71
  123.3 25.9 %copy-start.2 = (bf16[64,768]{1,0:T(8,128)(2,1)S(1)}, bf16[64,768]{1,0:T(8,128)(2,1)}, u32[]{:S(2)}) copy-start(bf16[64,768]{1,0:T(8,128)(2,1)} %param.9) | copy-start | bytes 294916
  123.5 59.4 %copy-start.3 = (bf16[2,2,512,64]{2,3,1,0:T(8,128)(2,1)S(1)}, bf16[2,2,512,64]{2,3,1,0:T(8,128)(2,1)}, u32[]{:S(2)}) copy-start(bf16[2,2,512,64]{2,3,1,0:T(8,128)(2,1)} %param.16) | copy-start | bytes 786436
  123.5 59.4 %copy-start.5 = (bf16[2,64,512]{2,1,0:T(8,128)(2,1)S(1)}, bf16[2,64,512]{2,1,0:T(8,128)(2,1)}, u32[]{:S(2)}) copy-start(bf16[2,64,512]{2,1,0:T(8,128)(2,1)} %param.17) | copy-start | bytes 393220
  149.9 76.0 %reduce-scatter.15.cloned.1.call-start = ((), (), s32[]{:S(2)}) async-start(), calls=%async_computation.11 | async-start | bytes 1769472
  248.9 13.9 %all-to-all-start.1 = ((bf16[32,2,1024]{2,1,0:T(2,128)(2,1)}), bf16[32,2,1024]{2,1,0:T(2,128)(2,1)S(1)}, u32[]{:S(2)}, u32[]{:S(2)}) async-start(bf16[32,2,1024]{2,1,0:T(2,128)(2,1)} %reshape.118), calls=%async_computation.1 | async-start | bytes 262144 | tf_op jit(solution)/shard_map/all_to_all | solution.py:54
  257.4 51.2 %all-gather.9.cloned.1.call-start = ((), (), s32[]{:S(2)}) async-start(), calls=%async_computation.8 | async-start | bytes 3538944 | tf_op jit(solution)/shard_map/all_gather | solution.py:31
  267.6 88.4 %reduce-scatter.17.cloned.1.call-start = ((), (), s32[]{:S(2)}) async-start(), calls=%async_computation.12 | async-start | bytes 2359296
  313.5 103.8 %all-gather.11.cloned.1.call-start = ((), (), s32[]{:S(2)}) async-start(), calls=%async_computation.9 | async-start | bytes 1769472 | tf_op jit(solution)/shard_map/all_gather | solution.py:71
  377.2 40.1 %copy-start.6 = (bf16[2,64,512]{2,1,0:T(8,128)(2,1)S(1)}, bf16[2,64,512]{2,1,0:T(8,128)(2,1)}, u32[]{:S(2)}) copy-start(bf16[2,64,512]{2,1,0:T(8,128)(2,1)} %param.17) | copy-start | bytes 393220
  384.4 76.2 %reduce-scatter.19.cloned.1.call-start = ((), (), s32[]{:S(2)}) async-start(), calls=%async_computation.13 | async-start | bytes 1769472
Sparse Core Ops, SparseCore 0:
  31.5 43.2 all-gather.4
  79.8 42.3 reduce-scatter.12
  150.1 32.8 all-gather.6
  186.9 39.0 reduce-scatter.14
  267.8 40.8 all-gather.8
  313.6 42.4 reduce-scatter.16
  384.5 32.7 all-gather.10
  421.3 39.2 reduce-scatter.18
where the time goes:
time: 488 us; the launch traced here: 487 us
  waiting for transfers between devices  317 us (65%)
  blocking collectives  69.1 us (14%)
  local copies, waits for them, and re-layouts  37.9 us (8%)
  other arithmetic  20.9 us (4%)
  starting transfers between devices  17.3 us (4%)
  between operations  14.6 us (3%)
  matrix products  10.2 us (2%)
    unnamed x12, waiting for transfers between devices  163 us
    all_gather x2, waiting for transfers between devices, edge_hidden(): lax.all_gather(stacked, 'ch', axis=1, tiled=True)  84.3 us
    psum x4, blocking collectives, finish(): lax.psum((jnp.sum(summed, axis=0), jnp.sum(summed * summed, axis=0)), 'ch')  69.1 us
    all_gather x2, waiting for transfers between devices, shards(): lax.all_gather(both, 'ch', axis=1, tiled=True)  65.8 us
    all_to_all x2, starting transfers between devices, shards(): lax.all_to_all(packed, 'dom', split_axis=1, concat_axis=1, tiled=True)  16.9 us
    unnamed x34, local copies, waits for them, and re-layouts  16.5 us
    gather x6, local copies, waits for them, and re-layouts, shards(): stacked = jnp.stack([edges, extended[:, edge_src], nodes[:, edge_dst]])  13.1 us
    scatter-add x2, other arithmetic, shards(): gathered = jnp.zeros((share, node_count), jnp.float32).at[:, edge_dst].ad...  12.3 us
  transfers between devices with their start and end apart: 10, of which 10 were waited for; matrix products, arithmetic and copies ran while one was open for 2% of the time, Pallas kernels for 0%

commit v1 on v0

--- a/solution.py
+++ b/solution.py
@@ -28,7 +28,9 @@
     return jnp.einsum(
         "akh,ake->he",
         weight_in,
-        lax.all_gather(stacked, "ch", axis=1, tiled=True),
+        jnp.concatenate(
+            lax.all_to_all(jnp.stack([stacked] * lax.axis_size("ch")), "ch", 0, 0), axis=1
+        ),
         preferred_element_type=jnp.float32,
     )
 

time: 488 us -> 559 us (1.15)
  blocking collectives: 69.1 us -> 230 us
  waiting for transfers between devices: 317 us -> 223 us
    all_to_all x0 -> x2, blocking collectives: none -> 162 us  [edge_hidden(): lax.all_to_all(jnp.stack([stacked] * lax.axis_size('ch')), 'ch', 0, 0)]
    all_gather x2 -> x0, waiting for transfers between devices: 84.3 us -> none  [edge_hidden(): lax.all_gather(stacked, 'ch', axis=1, tiled=True)]
    unnamed x12 -> x10, waiting for transfers between devices: 163 us -> 153 us
    unnamed x34 -> x44, local copies, waits for them, and re-layouts: 16.5 us -> 19.5 us
    gather x6 -> x4, local copies, waits for them, and re-layouts: 13.1 us -> 12.8 us  [shards(): stacked = jnp.stack([edges, extended[:, edge_src], nodes[:, edge_dst]])]
  transfers between devices with their start and end apart: 10 -> 8, of which waited for: 10 -> 8; matrix products, arithmetic and copies ran while one was open for 2% -> 1% of each run, Pallas kernels for 0% -> 0%
where the time goes in v1:
time: 559 us; the launch traced here: 558 us
  blocking collectives  230 us (41%)
  waiting for transfers between devices  223 us (40%)
  local copies, waits for them, and re-layouts  41.9 us (7%)
  other arithmetic  20.4 us (4%)
  starting transfers between devices  17.1 us (3%)
  between operations  14.6 us (3%)
  matrix products  10.9 us (2%)
    all_to_all x2, blocking collectives, edge_hidden(): lax.all_to_all(jnp.stack([stacked] * lax.axis_size('ch')), 'ch', 0, 0)  162 us
    unnamed x10, waiting for transfers between devices  153 us
    psum x4, blocking collectives, finish(): lax.psum((jnp.sum(summed, axis=0), jnp.sum(summed * summed, axis=0)), 'ch')  68.8 us
    all_gather x2, waiting for transfers between devices, shards(): lax.all_gather(both, 'ch', axis=1, tiled=True)  65.7 us
    unnamed x44, local copies, waits for them, and re-layouts  19.5 us
    all_to_all x2, starting transfers between devices, shards(): lax.all_to_all(packed, 'dom', split_axis=1, concat_axis=1, tiled=True)  16.8 us
    gather x4, local copies, waits for them, and re-layouts, shards(): stacked = jnp.stack([edges, extended[:, edge_src], nodes[:, edge_dst]])  12.8 us
    scatter-add x2, other arithmetic, shards(): gathered = jnp.zeros((share, node_count), jnp.float32).at[:, edge_dst].ad...  12.3 us
  transfers between devices with their start and end apart: 8, of which 8 were waited for; matrix products, arithmetic and copies ran while one was open for 1% of the time, Pallas kernels for 0%

profile of v1, /device:TPU:42, one launch (start us, length us, event | category | flops | bytes accessed | tf_op | source)
XLA Modules:
  0.0 557.9 jit_solution(8208312749045597225)
XLA Ops:
  7.2 0.7 fusion.44
  7.9 1.1 copy.23
  9.0 3.2 gather_fusion
  12.2 0.8 reshape.136
  13.0 8.4 %all-to-all-start = ((bf16[32,2,1024]{2,1,0:T(2,128)(2,1)}), bf16[32,2,1024]{2,1,0:T(2,128)(2,1)S(1)}, u32[]{:S(2)}, u32[]{:S(2)}) async-start(bf16[32,2,1024]{2,1,0:T(2,128)(2,1)} %reshape.136), calls=%async_computation | async-start | bytes 262144 | tf_op jit(solution)/shard_map/all_to_all | solution.py:56
  21.8 3.2 gather_fusion.2
  25.0 1.9 all-to-all-done
  27.2 3.2 gather_fusion.1
  31.3 81.9 %all_to_all.20 = bf16[8,3,64,1024]{3,2,1,0:T(8,128)(2,1)S(1)} all-to-all(bf16[8,3,64,1024]{3,2,1,0:T(8,128)(2,1)S(1)} %stack.69), channel_id=1, replica_groups=mesh['dom'=32,'ch'=8] {'ch'}, dimensions={0} | all-to-all | bytes 6291456 | tf_op jit(solution)/shard_map/all_to_all | solution.py:32
  114.1 3.2 convolution_bitcast_fusion.1
  117.4 2.9 copy.38
  120.4 37.4 %reduce-scatter.13.cloned.1.call-done = f32[64,1024]{1,0:T(8,128)} async-done(((f32[512,1024]{1,0:T(8,128)}), f32[64,1024]{1,0:T(8,128)}) %reduce-scatter.13.cloned.1.call-update) | async-done | bytes 262160
  157.9 1.1 copy.39
  159.2 1.0 reduce_sum.72
  160.2 18.2 %all-reduce.3 = (f32[1024]{0:T(1024)S(1)}, f32[1024]{0:T(1024)S(1)}) all-reduce(f32[1024]{0:T(1024)S(1)} %multiply_reduce_fusion.1, f32[1024]{0:T(1024)S(1)} %reduce_sum.72), channel_id=1, replica_groups=mesh['dom'=32,'ch'=8] {'ch'}, use_global_device_ids=true, to_apply=%region_4.5 | all-reduce | flops 2048 | bytes 16384 | tf_op jit(solution)/shard_map/psum | solution.py:20
  178.8 6.2 %scatter_custom_fusion = f32[64,768]{0,1:T(8,128)S(1)} fusion(s32[1024]{0:T(1024)S(1)} %get-tuple-element.23, bf16[64,1024]{0,1:T(8,128)(2,1)S(1)} %add_convert_fusion, f32[]{:T(128)} %constant.23.clone.1), kind=kCustom, calls=%fused_computation.22 | custom fusion | flops 131072 | bytes 458756 | tf_op jit(solution)/shard_map/scatter-add | solution.py:66
  185.1 0.7 pad_maximum_fusion.5
  185.9 32.7 %all-gather.3.cloned.1.call-done = bf16[2,512,768]{2,1,0:T(8,128)(2,1)} async-done(((bf16[2,64,768]{2,1,0:T(8,128)(2,1)}), bf16[2,512,768]{2,1,0:T(8,128)(2,1)}) %all-gather.3.cloned.1.call-update) | async-done | bytes 1572880 | tf_op jit(solution)/shard_map/all_gather | solution.py:73
  218.6 2.2 convolution_bitcast_fusion.3
  220.8 1.6 copy.40
  222.5 39.2 %reduce-scatter.15.cloned.1.call-done = f32[64,768]{1,0:T(8,128)} async-done(((f32[512,768]{1,0:T(8,128)}), f32[64,768]{1,0:T(8,128)}) %reduce-scatter.15.cloned.1.call-update) | async-done | bytes 196624
  261.7 1.1 copy.41
  263.0 1.0 reduce_sum.74
  263.9 16.3 %all-reduce.2 = (f32[768]{0:T(1024)S(1)}, f32[768]{0:T(1024)S(1)}) all-reduce(f32[768]{0:T(1024)S(1)} %multiply_reduce_fusion.3, f32[768]{0:T(1024)S(1)} %reduce_sum.74), channel_id=1, replica_groups=mesh['dom'=32,'ch'=8] {'ch'}, use_global_device_ids=true, to_apply=%region_10.11 | all-reduce | flops 1536 | bytes 12288 | tf_op jit(solution)/shard_map/psum | solution.py:20
  280.5 3.2 gather_fusion.3
  283.7 0.8 reshape.138
  284.6 8.4 %all-to-all-start.2 = ((bf16[32,2,1024]{2,1,0:T(2,128)(2,1)}), bf16[32,2,1024]{2,1,0:T(2,128)(2,1)S(1)}, u32[]{:S(2)}, u32[]{:S(2)}) async-start(bf16[32,2,1024]{2,1,0:T(2,128)(2,1)} %reshape.138), calls=%async_computation.2 | async-start | bytes 262144 | tf_op jit(solution)/shard_map/all_to_all | solution.py:56
  293.0 3.2 gather_fusion.5
  296.3 2.2 all-to-all-done.2
  298.7 3.2 gather_fusion.4
  302.8 79.8 %all_to_all.21 = bf16[8,3,64,1024]{3,2,1,0:T(8,128)(2,1)S(1)} all-to-all(bf16[8,3,64,1024]{3,2,1,0:T(8,128)(2,1)S(1)} %stack.77), channel_id=1, replica_groups=mesh['dom'=32,'ch'=8] {'ch'}, dimensions={0} | all-to-all | bytes 6291456 | tf_op jit(solution)/shard_map/all_to_all | solution.py:32
  383.5 3.2 convolution_bitcast_fusion
  386.8 2.9 copy.42
  389.8 37.6 %reduce-scatter.17.cloned.1.call-done = f32[64,1024]{1,0:T(8,128)} async-done(((f32[512,1024]{1,0:T(8,128)}), f32[64,1024]{1,0:T(8,128)}) %reduce-scatter.17.cloned.1.call-update) | async-done | bytes 262160
  427.4 1.1 copy.43
  428.8 1.0 reduce_sum.76
  429.8 17.9 %all-reduce.1 = (f32[1024]{0:T(1024)S(1)}, f32[1024]{0:T(1024)S(1)}) all-reduce(f32[1024]{0:T(1024)S(1)} %multiply_reduce_fusion, f32[1024]{0:T(1024)S(1)} %reduce_sum.76), channel_id=1, replica_groups=mesh['dom'=32,'ch'=8] {'ch'}, use_global_device_ids=true, to_apply=%region_15.16 | all-reduce | flops 2048 | bytes 16384 | tf_op jit(solution)/shard_map/psum | solution.py:20
  448.1 6.2 %scatter_custom_fusion.1 = f32[64,768]{0,1:T(8,128)S(1)} fusion(s32[1024]{0:T(1024)S(1)} %get-tuple-element.23, bf16[64,1024]{0,1:T(8,128)(2,1)S(1)} %fusion.6, f32[]{:T(128)} %constant.23.clone.1), kind=kCustom, calls=%fused_computation.24 | custom fusion | flops 131072 | bytes 458756 | tf_op jit(solution)/shard_map/scatter-add | solution.py:66
  454.3 0.9 copy.34
  455.3 33.0 %all-gather.5.cloned.1.call-done = bf16[2,512,768]{2,0,1:T(2,128)(2,1)} async-done(((bf16[2,64,768]{2,0,1:T(2,128)(2,1)}), bf16[2,512,768]{2,0,1:T(2,128)(2,1)}) %all-gather.5.cloned.1.call-update) | async-done | bytes 1572880 | tf_op jit(solution)/shard_map/all_gather | solution.py:73
  488.2 2.2 convolution_bitcast_fusion.2
  490.5 1.6 copy.44
  492.1 0.8 copy.37
  492.9 38.5 %reduce-scatter.19.cloned.1.call-done = f32[64,768]{1,0:T(8,128)} async-done(((f32[512,768]{1,0:T(8,128)}), f32[64,768]{1,0:T(8,128)}) %reduce-scatter.19.cloned.1.call-update) | async-done | bytes 196624
  531.4 1.1 copy.45
  532.6 1.0 reduce_sum.78
  533.6 16.4 %all-reduce = (f32[768]{0:T(1024)S(1)}, f32[768]{0:T(1024)S(1)}) all-reduce(f32[768]{0:T(1024)S(1)} %multiply_reduce_fusion.2, f32[768]{0:T(1024)S(1)} %reduce_sum.78), channel_id=1, replica_groups=mesh['dom'=32,'ch'=8] {'ch'}, use_global_device_ids=true, to_apply=%region_21.22 | all-reduce | flops 1536 | bytes 12288 | tf_op jit(solution)/shard_map/psum | solution.py:20
  550.3 0.8 copy.36
  (70 shorter events, 6.9 us)
Async XLA Ops:
  7.2 14.4 %copy-start.12 = (s32[1024]{0:T(1024)S(1)}, s32[1024]{0:T(1024)}, u32[]{:S(2)}) copy-start(s32[1024]{0:T(1024)} %param.13) | copy-start | bytes 12292
  7.2 14.4 %copy-start.9 = (bf16[64,1024]{1,0:T(8,128)(2,1)S(1)}, bf16[64,1024]{1,0:T(8,128)(2,1)}, u32[]{:S(2)}) copy-start(bf16[64,1024]{1,0:T(8,128)(2,1)} %param.10) | copy-start | bytes 393220
  7.2 17.8 %copy-start.13 = (s32[1024]{0:T(1024)S(1)}, s32[1024]{0:T(1024)}, u32[]{:S(2)}) copy-start(s32[1024]{0:T(1024)} %param.12) | copy-start | bytes 12292
  13.0 13.9 %all-to-all-start = ((bf16[32,2,1024]{2,1,0:T(2,128)(2,1)}), bf16[32,2,1024]{2,1,0:T(2,128)(2,1)S(1)}, u32[]{:S(2)}, u32[]{:S(2)}) async-start(bf16[32,2,1024]{2,1,0:T(2,128)(2,1)} %reshape.136), calls=%async_computation | async-start | bytes 262144 | tf_op jit(solution)/shard_map/all_to_all | solution.py:56
  21.5 136.4 %reduce-scatter.13.cloned.1.call-start = ((), (), s32[]{:S(2)}) async-start(), calls=%async_computation.10 | async-start | bytes 2359296
  21.7 8.9 %copy-start.2 = (bf16[64,1024]{0,1:T(8,128)(2,1)}, bf16[64,1024]{0,1:T(8,128)(2,1)S(1)}, u32[]{:S(2)}) copy-start(bf16[64,1024]{0,1:T(8,128)(2,1)S(1)} %copy.24) | copy-start | bytes 393220
  113.2 0.9 copy-start.7
  120.3 58.1 %copy-start.3 = (bf16[64,1024]{0,1:T(8,128)(2,1)S(1)}, bf16[64,1024]{0,1:T(8,128)(2,1)}, u32[]{:S(2)}) copy-start(bf16[64,1024]{0,1:T(8,128)(2,1)} %copy-done.2) | copy-start | bytes 393220
  120.4 64.8 %copy-start.4 = (bf16[64,768]{1,0:T(8,128)(2,1)S(1)}, bf16[64,768]{1,0:T(8,128)(2,1)}, u32[]{:S(2)}) copy-start(bf16[64,768]{1,0:T(8,128)(2,1)} %param.9) | copy-start | bytes 294916
  120.4 98.2 %copy-start.5 = (bf16[2,2,512,64]{2,3,1,0:T(8,128)(2,1)S(1)}, bf16[2,2,512,64]{2,3,1,0:T(8,128)(2,1)}, u32[]{:S(2)}) copy-start(bf16[2,2,512,64]{2,3,1,0:T(8,128)(2,1)} %param.16) | copy-start | bytes 786436
  120.4 98.2 %copy-start.10 = (bf16[2,64,512]{2,1,0:T(8,128)(2,1)S(1)}, bf16[2,64,512]{2,1,0:T(8,128)(2,1)}, u32[]{:S(2)}) copy-start(bf16[2,64,512]{2,1,0:T(8,128)(2,1)} %param.17) | copy-start | bytes 393220
  120.4 98.2 %all-gather.3.cloned.1.call-start = ((), (), s32[]{:S(2)}) async-start(), calls=%async_computation.8 | async-start | bytes 1769472 | tf_op jit(solution)/shard_map/all_gather | solution.py:73
  178.8 123.1 %copy-start = (bf16[64,1024]{0,1:T(8,128)(2,1)}, bf16[64,1024]{0,1:T(8,128)(2,1)S(1)}, u32[]{:S(2)}) copy-start(bf16[64,1024]{0,1:T(8,128)(2,1)S(1)} %add_convert_fusion) | copy-start | bytes 393220
  185.8 75.9 %reduce-scatter.15.cloned.1.call-start = ((), (), s32[]{:S(2)}) async-start(), calls=%async_computation.11 | async-start | bytes 1769472
  284.6 13.8 %all-to-all-start.2 = ((bf16[32,2,1024]{2,1,0:T(2,128)(2,1)}), bf16[32,2,1024]{2,1,0:T(2,128)(2,1)S(1)}, u32[]{:S(2)}, u32[]{:S(2)}) async-start(bf16[32,2,1024]{2,1,0:T(2,128)(2,1)} %reshape.138), calls=%async_computation.2 | async-start | bytes 262144 | tf_op jit(solution)/shard_map/all_to_all | solution.py:56
  293.0 134.4 %reduce-scatter.17.cloned.1.call-start = ((), (), s32[]{:S(2)}) async-start(), calls=%async_computation.12 | async-start | bytes 2359296
  382.6 0.9 copy-start.8
  389.7 58.0 %copy-start.1 = (bf16[64,1024]{0,1:T(8,128)(2,1)S(1)}, bf16[64,1024]{0,1:T(8,128)(2,1)}, u32[]{:S(2)}) copy-start(bf16[64,1024]{0,1:T(8,128)(2,1)} %copy-done) | copy-start | bytes 393220
  389.7 98.5 %all-gather.5.cloned.1.call-start = ((), (), s32[]{:S(2)}) async-start(), calls=%async_computation.9 | async-start | bytes 1769472 | tf_op jit(solution)/shard_map/all_gather | solution.py:73
  428.8 59.5 %copy-start.6 = (bf16[2,2,512,64]{2,3,1,0:T(8,128)(2,1)S(1)}, bf16[2,2,512,64]{2,3,1,0:T(8,128)(2,1)}, u32[]{:S(2)}) copy-start(bf16[2,2,512,64]{2,3,1,0:T(8,128)(2,1)} %param.16) | copy-start | bytes 786436
  428.8 59.5 %copy-start.11 = (bf16[2,64,512]{2,1,0:T(8,128)(2,1)S(1)}, bf16[2,64,512]{2,1,0:T(8,128)(2,1)}, u32[]{:S(2)}) copy-start(bf16[2,64,512]{2,1,0:T(8,128)(2,1)} %param.17) | copy-start | bytes 393220
  455.2 76.1 %reduce-scatter.19.cloned.1.call-start = ((), (), s32[]{:S(2)}) async-start(), calls=%async_computation.13 | async-start | bytes 1769472
Sparse Core Ops, SparseCore 0:
  120.5 37.3 reduce-scatter.12
  186.0 32.6 all-gather.2
  222.6 39.0 reduce-scatter.14
  389.8 37.4 reduce-scatter.16
  455.3 32.8 all-gather.4
  492.2 39.0 reduce-scatter.18
